TPU v7x, 128 devices: a whole 4x4x4 slice. The times are simulated.
128 devices in a mesh: row: 4 (over x_lo, core), col: 8 (over x_hi, y), tm: 4 (over z).
Axes of the slice: x: 4 (x_hi: 2, x_lo: 2; x = x_hi * 2 + x_lo), y: 4, z: 4, core: 2. Of those that a mesh axis runs over, the one named last changes fastest.
Arguments:
- right_sides: bfloat16 [8, 256, 16384], P(None, 'tm', ('row', 'col')), may hold values from -6 to 6
- eigen_basis: bfloat16 [16384, 16384], P('row', 'col'), may hold values from -0.046875 to 0.046875
- space_values: float32 [16384], P('col'), may hold values from 0.02 to 4
- time_basis: bfloat16 [256, 256], replicated, may hold values from -0.375 to 0.375
- time_values: float32 [256], replicated, may hold values from 0.05 to 4
- noise_level: float32 [1], replicated, may hold values from 0.05 to 0.5
Outputs:
- solved: float32 [8, 256, 16384], P(None, 'tm', ('row', 'col'))
All inputs are finite; a program needn't handle non-finite values.
Results may differ from a plain program's by a relative error of at most 0.0037.
Values may be sent and summed in bfloat16 or wider, within the bound.
No kernel may reach another device: no remote copies, remote signals or barrier semaphores. Data moves between devices by JAX's collectives and lax.ppermute only.
A program may use at most 128 MiB of HBM per device.

v0:
```python
import jax
import jax.numpy as jnp
from jax import lax
from jax.sharding import PartitionSpec as P


def shards(right_sides, eigen_basis, space_values, time_basis, time_values, noise_level):
    span = space_values.shape[0] // lax.axis_size("tm")
    value_part = lax.dynamic_slice_in_dim(space_values, lax.axis_index("tm") * span, span, 0)
    partial_value = jnp.einsum(
        "rts,si->rti",
        lax.all_gather(right_sides, "col", axis=2, tiled=True),
        eigen_basis,
        preferred_element_type=jnp.float32,
    )
    spectral = lax.psum(partial_value, "row").astype(jnp.bfloat16)
    mixed = jnp.einsum(
        "tj,kti->kji",
        time_basis,
        lax.all_to_all(spectral, "tm", split_axis=2, concat_axis=1, tiled=True),
        preferred_element_type=jnp.float32,
    )
    denom = value_part[None, None, :] * time_values[None, :, None] + noise_level[0]
    scaled = (mixed / denom).astype(jnp.bfloat16)
    own_part = lax.all_to_all(
        jnp.einsum("tj,kji->kti", time_basis, scaled, preferred_element_type=jnp.float32).astype(
            jnp.bfloat16
        ),
        "tm",
        split_axis=1,
        concat_axis=2,
        tiled=True,
    )
    terms = jnp.einsum("rti,si->rts", own_part, eigen_basis, preferred_element_type=jnp.float32)
    return lax.psum_scatter(terms, "col", scatter_dimension=2, tiled=True)


def solution(mesh):
    placed = (P(None, "tm", ("row", "col")), P("row", "col"), P("col"), P(), P(), P())
    return jax.shard_map(
        shards, mesh=mesh, in_specs=placed, out_specs=P(None, "tm", ("row", "col")), check_vma=False
    )
```

profile of v0, /device:TPU:1, one launch (start us, length us, event | category | flops | bytes accessed | tf_op | source)
XLA Modules:
  0.0 404.2 jit_solution(12070897886368147849)
XLA Ops:
  6.5 0.0 copy-start
  6.5 0.0 all-gather.2.cloned.1.call-start
  6.5 0.7 all-gather.2.cloned.1.call-update
  7.3 78.7 %all-gather.2.cloned.1.call-done = bf16[8,64,4096]{2,1,0:T(8,128)(2,1)} async-done(((bf16[8,64,512]{2,1,0:T(8,128)(2,1)}), bf16[8,64,4096]{2,1,0:T(8,128)(2,1)}) %all-gather.2.cloned.1.call-update) | async-done | bytes 4194320 | tf_op jit(solution)/shard_map/all_gather | solution.py:12
  85.9 15.0 %fusion.2 = f32[8,64,2048]{2,1,0:T(8,128)} fusion(bf16[8,64,4096]{2,1,0:T(8,128)(2,1)} %all-gather.2.cloned.1.call-done, bf16[4096,2048]{1,0:T(8,128)(2,1)} %param.7), kind=kOutput, calls=%fused_computation.2 | convolution fusion | flops 8589934592 | bytes 25165824 | tf_op jit(solution)/shard_map/rts,si->rti/dot_general | solution.py:10
  101.0 77.3 %all-reduce.1 = bf16[8,64,2048]{2,1,0:T(8,128)(2,1)S(1)} all-reduce(f32[8,64,2048]{2,1,0:T(8,128)} %fusion.2), channel_id=1, replica_groups=mesh['row'=4,'col'=8,'tm'=4] {'row'}, use_global_device_ids=true, to_apply=%region_0.0 | all-reduce | flops 1048576 | bytes 6291456 | tf_op jit(solution)/shard_map/psum | solution.py:16
  178.3 4.3 %copy.16 = bf16[8,64,2048]{1,0,2:T(8,128)(2,1)} copy(bf16[8,64,2048]{2,1,0:T(8,128)(2,1)S(1)} %all-reduce.1) | data formatting | bytes 4194304 | tf_op jit(solution)/shard_map/convert_element_type | solution.py:16
  182.6 0.0 copy-start.1
  182.6 5.9 %reshape.36 = bf16[4,2,131072]{2,1,0:T(2,128)(2,1)} reshape(bf16[2048,8,64]{2,1,0:T(8,128)(2,1)} %bitcast.30) | data formatting | bytes 4194304
  188.5 4.1 %all-to-all-start = ((bf16[4,2,131072]{2,1,0:T(2,128)(2,1)}), bf16[4,2,131072]{2,1,0:T(2,128)(2,1)S(1)}, u32[]{:S(2)}, u32[]{:S(2)}) async-start(bf16[4,2,131072]{2,1,0:T(2,128)(2,1)} %reshape.36), calls=%async_computation | async-start | bytes 4194304 | tf_op jit(solution)/shard_map/all_to_all | solution.py:20
  192.6 0.0 reduce-scatter.2.cloned.1.call-start
  193.3 0.8 dynamic_slice.3
  194.1 0.0 copy-done.1
  194.1 0.1 multiply_add_fusion
  194.2 24.4 %all-to-all-done = bf16[4,2,131072]{2,1,0:T(2,128)(2,1)S(1)} async-done(((bf16[4,2,131072]{2,1,0:T(2,128)(2,1)}), bf16[4,2,131072]{2,1,0:T(2,128)(2,1)S(1)}, u32[]{:S(2)}, u32[]{:S(2)}) %all-to-all-start) | async-done | bytes 2097184 | tf_op jit(solution)/shard_map/all_to_all | solution.py:20
  218.6 4.0 reshape.37
  222.6 5.2 %copy.24 = bf16[8,64,4,512]{3,2,1,0:T(4,128)(2,1)S(1)} copy(bf16[8,64,4,512]{1,0,3,2:T(8,128)(2,1)} %bitcast.31) | data formatting | bytes 4194304 | tf_op jit(solution)/shard_map/all_to_all | solution.py:20
  227.8 1.9 copy.18
  229.7 0.0 copy-done
  229.7 5.0 %convert_bitcast_fusion = bf16[8,256,512]{1,2,0:T(8,128)(2,1)} fusion(bf16[8,256,512]{2,1,0:T(8,128)(2,1)} %bitcast.34, f32[256,512]{0,1:T(8,128)S(1)} %multiply_add_fusion, bf16[256,256]{1,0:T(8,128)(2,1)S(1)} %copy-done), kind=kOutput, calls=%fused_computation.6 | convolution fusion | flops 1076887552 | bytes 4849664 | tf_op jit(solution)/shard_map/tj,kji->kti/dot_general | solution.py:26
  234.7 3.4 copy.20
  238.0 27.3 %all_to_all.36 = bf16[8,256,512]{2,0,1:T(8,128)(2,1)S(1)} all-to-all(bf16[8,256,512]{2,0,1:T(8,128)(2,1)S(1)} %copy.20), channel_id=1, replica_groups=mesh['row'=4,'col'=8,'tm'=4] {'tm'}, dimensions={1} | all-to-all | bytes 4194304 | tf_op jit(solution)/shard_map/all_to_all | solution.py:25
  265.3 1.6 copy.22
  266.9 2.8 all_to_all.33
  269.7 15.1 %fusion = f32[8,64,4096]{2,1,0:T(8,128)} fusion(bf16[8,64,2048]{2,1,0:T(8,128)(2,1)} %all_to_all.33, bf16[4096,2048]{1,0:T(8,128)(2,1)} %param.7), kind=kOutput, calls=%fused_computation | convolution fusion | flops 8589934592 | bytes 27262976 | tf_op jit(solution)/shard_map/rti,si->rts/dot_general | solution.py:34
  284.8 0.0 reduce-scatter.2.cloned.1.call-update
  284.9 112.5 %reduce-scatter.2.cloned.1.call-done = f32[8,64,512]{2,1,0:T(8,128)} async-done(((f32[8,64,4096]{2,1,0:T(8,128)}), f32[8,64,512]{2,1,0:T(8,128)}) %reduce-scatter.2.cloned.1.call-update) | async-done | bytes 1048592 | tf_op jit(solution)/shard_map/reduce_scatter | solution.py:35
Async XLA Ops:
  6.5 223.1 %copy-start = (bf16[256,256]{1,0:T(8,128)(2,1)S(1)}, bf16[256,256]{1,0:T(8,128)(2,1)}, u32[]{:S(2)}) copy-start(bf16[256,256]{1,0:T(8,128)(2,1)} %param.9) | copy-start | bytes 393220
  6.5 79.4 %all-gather.2.cloned.1.call-start = ((), (), s32[]{:S(2)}) async-start(), calls=%async_computation.3 | async-start | bytes 4718592 | tf_op jit(solution)/shard_map/all_gather | solution.py:12
  182.6 11.5 %copy-start.1 = (f32[256]{0:T(256)S(1)}, f32[256]{0:T(256)}, u32[]{:S(2)}) copy-start(f32[256]{0:T(256)} %param.10) | copy-start | bytes 3076
  188.5 30.1 %all-to-all-start = ((bf16[4,2,131072]{2,1,0:T(2,128)(2,1)}), bf16[4,2,131072]{2,1,0:T(2,128)(2,1)S(1)}, u32[]{:S(2)}, u32[]{:S(2)}) async-start(bf16[4,2,131072]{2,1,0:T(2,128)(2,1)} %reshape.36), calls=%async_computation | async-start | bytes 4194304 | tf_op jit(solution)/shard_map/all_to_all | solution.py:20
  192.6 204.7 %reduce-scatter.2.cloned.1.call-start = ((), (), s32[]{:S(2)}) async-start(), calls=%async_computation.4 | async-start | bytes 9437184 | tf_op jit(solution)/shard_map/reduce_scatter | solution.py:35
Sparse Core Ops, SparseCore 0:
  9.5 76.3 all-gather.1
  285.0 112.3 reduce-scatter.1
where the time goes:
time: 405 us; the launch traced here: 404 us
  waiting for transfers between devices  216 us (53%)
  blocking collectives  105 us (26%)
  matrix products  35.1 us (9%)
  local copies, waits for them, and re-layouts  29.8 us (7%)
  between operations  14.1 us (3%)
  starting transfers between devices  4.14 us (1%)
    reduce_scatter x1, waiting for transfers between devices, shards(): return lax.psum_scatter(terms, 'col', scatter_dimension=2, tiled=True)  112 us
    all_gather x1, waiting for transfers between devices, shards(): lax.all_gather(right_sides, 'col', axis=2, tiled=True)  78.7 us
    psum x1, blocking collectives, shards(): spectral = lax.psum(partial_value, 'row').astype(jnp.bfloat16)  77.3 us
    all_to_all x1, blocking collectives, shards(): lax.all_to_all(jnp.einsum('tj,kji->kti', time_basis, scaled, preferred_el...  27.3 us
    all_to_all x1, waiting for transfers between devices, shards(): lax.all_to_all(spectral, 'tm', split_axis=2, concat_axis=1, tiled=True)  24.4 us
    dot_general x1, matrix products, shards(): jnp.einsum('rti,si->rts', own_part, eigen_basis, preferred_element_type=j...  15.1 us
    dot_general x1, matrix products, shards(): jnp.einsum('rts,si->rti', lax.all_gather(right_sides, 'col', axis=2, tile...  15 us
    unnamed x6, local copies, waits for them, and re-layouts  9.92 us
  transfers between devices with their start and end apart: 3, of which 3 were waited for; matrix products, arithmetic and copies ran while one was open for 0% of the time, Pallas kernels for 0%

commit v1 on v0

--- a/solution.py
+++ b/solution.py
@@ -13,7 +13,7 @@
         eigen_basis,
         preferred_element_type=jnp.float32,
     )
-    spectral = lax.psum(partial_value, "row").astype(jnp.bfloat16)
+    spectral = jnp.sum(lax.all_gather(partial_value, "row"), axis=0).astype(jnp.bfloat16)
     mixed = jnp.einsum(
         "tj,kti->kji",
         time_basis,

time: 405 us -> 488 us (1.20)
  waiting for transfers between devices: 216 us -> 367 us
  blocking collectives: 105 us -> 28.7 us
  other arithmetic: 0.13 us -> 8.32 us
    all_gather x0 -> x1, waiting for transfers between devices: none -> 150 us  [shards(): lax.all_gather(partial_value, 'row')]
    psum x1 -> x0, blocking collectives: 77.3 us -> none  [shards(): spectral = lax.psum(partial_value, 'row').astype(jnp.bfloat16)]
    reduce_sum x0 -> x1, other arithmetic: none -> 8.19 us  [shards(): jnp.sum(lax.all_gather(partial_value, 'row'), axis=0).astype(jnp.bfloat16)]
    unnamed x6 -> x8, local copies, waits for them, and re-layouts: 9.92 us -> 9.92 us
  transfers between devices with their start and end apart: 3 -> 4, of which waited for: 3 -> 4; matrix products, arithmetic and copies ran while one was open for 0% -> 0% of each run, Pallas kernels for 0% -> 0%
where the time goes in v1:
time: 488 us; the launch traced here: 487 us
  waiting for transfers between devices  367 us (75%)
  matrix products  35 us (7%)
  local copies, waits for them, and re-layouts  29.8 us (6%)
  blocking collectives  28.7 us (6%)
  between operations  13.8 us (3%)
  other arithmetic  8.32 us (2%)
    all_gather x1, waiting for transfers between devices, shards(): lax.all_gather(partial_value, 'row')  150 us
    reduce_scatter x1, waiting for transfers between devices, shards(): return lax.psum_scatter(terms, 'col', scatter_dimension=2, tiled=True)  114 us
    all_gather x1, waiting for transfers between devices, shards(): lax.all_gather(right_sides, 'col', axis=2, tiled=True)  78.6 us
    all_to_all x1, blocking collectives, shards(): lax.all_to_all(jnp.einsum('tj,kji->kti', time_basis, scaled, preferred_el...  28.7 us
    all_to_all x1, waiting for transfers between devices, shards(): lax.all_to_all(spectral, 'tm', split_axis=2, concat_axis=1, tiled=True)  24.3 us
    dot_general x1, matrix products, shards(): jnp.einsum('rti,si->rts', own_part, eigen_basis, preferred_element_type=j...  15 us
    dot_general x1, matrix products, shards(): jnp.einsum('rts,si->rti', lax.all_gather(right_sides, 'col', axis=2, tile...  15 us
    unnamed x8, local copies, waits for them, and re-layouts  9.92 us
  transfers between devices with their start and end apart: 4, of which 4 were waited for; matrix products, arithmetic and copies ran while one was open for 0% of the time, Pallas kernels for 0%

profile of v1, /device:TPU:1, one launch (start us, length us, event | category | flops | bytes accessed | tf_op | source)
XLA Modules:
  0.0 487.1 jit_solution(9430651966808080916)
XLA Ops:
  6.5 0.0 copy-start
  6.5 0.0 all-gather.4.cloned.1.call-start
  6.5 0.7 all-gather.4.cloned.1.call-update
  7.3 0.0 all-gather.6.cloned.1.call-start
  7.3 78.6 %all-gather.4.cloned.1.call-done = bf16[8,64,4096]{2,1,0:T(8,128)(2,1)} async-done(((bf16[8,64,512]{2,1,0:T(8,128)(2,1)}), bf16[8,64,4096]{2,1,0:T(8,128)(2,1)}) %all-gather.4.cloned.1.call-update) | async-done | bytes 4194320 | tf_op jit(solution)/shard_map/all_gather | solution.py:12
  85.9 15.0 %fusion.2 = f32[8,64,2048]{2,1,0:T(8,128)} fusion(bf16[8,64,4096]{2,1,0:T(8,128)(2,1)} %all-gather.4.cloned.1.call-done, bf16[4096,2048]{1,0:T(8,128)(2,1)} %param.7), kind=kOutput, calls=%fused_computation.2 | convolution fusion | flops 8589934592 | bytes 25165824 | tf_op jit(solution)/shard_map/rts,si->rti/dot_general | solution.py:10
  100.9 0.0 all-gather.6.cloned.1.call-update
  101.0 150.0 %all-gather.6.cloned.1.call-done = f32[32,64,2048]{2,1,0:T(8,128)} async-done(((f32[8,64,2048]{2,1,0:T(8,128)}), f32[32,64,2048]{2,1,0:T(8,128)}) %all-gather.6.cloned.1.call-update) | async-done | bytes 16777232 | tf_op jit(solution)/shard_map/all_gather | solution.py:16
  251.0 8.2 %reduce_sum.9 = bf16[8,64,2048]{2,1,0:T(8,128)(2,1)S(1)} reduce(f32[4,8,64,2048]{3,2,1,0:T(8,128)} %bitcast.33, f32[]{:T(128)} %constant.5.clone.1), dimensions={0}, to_apply=%region_0.0 | reduce | flops 3145728 | bytes 18874372 | tf_op jit(solution)/shard_map/reduce_sum | solution.py:16
  259.2 4.3 copy.20
  263.5 0.0 copy-start.2
  263.5 5.9 %reshape.37 = bf16[4,2,131072]{2,1,0:T(2,128)(2,1)} reshape(bf16[2048,8,64]{2,1,0:T(8,128)(2,1)} %bitcast.31) | data formatting | bytes 4194304
  269.4 4.1 all-to-all-start
  273.5 0.0 reduce-scatter.2.cloned.1.call-start
  274.2 0.8 dynamic_slice.3
  275.0 0.0 copy-done.2
  275.0 0.1 multiply_add_fusion
  275.1 24.3 %all-to-all-done = bf16[4,2,131072]{2,1,0:T(2,128)(2,1)S(1)} async-done(((bf16[4,2,131072]{2,1,0:T(2,128)(2,1)}), bf16[4,2,131072]{2,1,0:T(2,128)(2,1)S(1)}, u32[]{:S(2)}, u32[]{:S(2)}) %all-to-all-start) | async-done | bytes 2097184 | tf_op jit(solution)/shard_map/all_to_all | solution.py:20
  299.4 4.0 reshape.38
  303.4 5.2 %copy.28 = bf16[8,64,4,512]{3,2,1,0:T(4,128)(2,1)S(1)} copy(bf16[8,64,4,512]{1,0,3,2:T(8,128)(2,1)} %bitcast.32) | data formatting | bytes 4194304 | tf_op jit(solution)/shard_map/all_to_all | solution.py:20
  308.6 1.9 copy.22
  310.5 0.0 copy-done
  310.5 5.0 %convert_bitcast_fusion = bf16[8,256,512]{1,2,0:T(8,128)(2,1)} fusion(bf16[8,256,512]{2,1,0:T(8,128)(2,1)} %bitcast.36, f32[256,512]{0,1:T(8,128)S(1)} %multiply_add_fusion, bf16[256,256]{1,0:T(8,128)(2,1)S(1)} %copy-done), kind=kOutput, calls=%fused_computation.6 | convolution fusion | flops 1076887552 | bytes 4849664 | tf_op jit(solution)/shard_map/tj,kji->kti/dot_general | solution.py:26
  315.5 3.4 copy.24
  318.8 28.7 %all_to_all.36 = bf16[8,256,512]{2,0,1:T(8,128)(2,1)S(1)} all-to-all(bf16[8,256,512]{2,0,1:T(8,128)(2,1)S(1)} %copy.24), channel_id=1, replica_groups=mesh['row'=4,'col'=8,'tm'=4] {'tm'}, dimensions={1} | all-to-all | bytes 4194304 | tf_op jit(solution)/shard_map/all_to_all | solution.py:25
  347.5 1.6 copy.26
  349.1 2.8 all_to_all.33
  352.0 15.0 %fusion = f32[8,64,4096]{2,1,0:T(8,128)} fusion(bf16[8,64,2048]{2,1,0:T(8,128)(2,1)} %all_to_all.33, bf16[4096,2048]{1,0:T(8,128)(2,1)} %param.7), kind=kOutput, calls=%fused_computation | convolution fusion | flops 8589934592 | bytes 27262976 | tf_op jit(solution)/shard_map/rti,si->rts/dot_general | solution.py:34
  367.0 0.0 copy-start.1
  367.0 0.0 reduce-scatter.2.cloned.1.call-update
  367.0 113.6 %reduce-scatter.2.cloned.1.call-done = f32[8,64,512]{2,1,0:T(8,128)} async-done(((f32[8,64,4096]{2,1,0:T(8,128)}), f32[8,64,512]{2,1,0:T(8,128)}) %reduce-scatter.2.cloned.1.call-update) | async-done | bytes 1048592 | tf_op jit(solution)/shard_map/reduce_scatter | solution.py:35
  480.6 0.0 copy-done.1
Async XLA Ops:
  6.5 303.9 %copy-start = (bf16[256,256]{1,0:T(8,128)(2,1)S(1)}, bf16[256,256]{1,0:T(8,128)(2,1)}, u32[]{:S(2)}) copy-start(bf16[256,256]{1,0:T(8,128)(2,1)} %param.9) | copy-start | bytes 393220
  6.5 79.4 %all-gather.4.cloned.1.call-start = ((), (), s32[]{:S(2)}) async-start(), calls=%async_computation.3 | async-start | bytes 4718592 | tf_op jit(solution)/shard_map/all_gather | solution.py:12
  7.3 243.7 %all-gather.6.cloned.1.call-start = ((), (), s32[]{:S(2)}) async-start(), calls=%async_computation.5 | async-start | bytes 20971520 | tf_op jit(solution)/shard_map/all_gather | solution.py:16
  263.5 11.5 %copy-start.2 = (f32[256]{0:T(256)S(1)}, f32[256]{0:T(256)}, u32[]{:S(2)}) copy-start(f32[256]{0:T(256)} %param.10) | copy-start | bytes 3076
  269.4 30.0 %all-to-all-start = ((bf16[4,2,131072]{2,1,0:T(2,128)(2,1)}), bf16[4,2,131072]{2,1,0:T(2,128)(2,1)S(1)}, u32[]{:S(2)}, u32[]{:S(2)}) async-start(bf16[4,2,131072]{2,1,0:T(2,128)(2,1)} %reshape.37), calls=%async_computation | async-start | bytes 4194304 | tf_op jit(solution)/shard_map/all_to_all | solution.py:20
  273.5 207.1 %reduce-scatter.2.cloned.1.call-start = ((), (), s32[]{:S(2)}) async-start(), calls=%async_computation.4 | async-start | bytes 9437184 | tf_op jit(solution)/shard_map/reduce_scatter | solution.py:35
  367.0 113.6 %copy-start.1 = (bf16[256,256]{1,0:T(8,128)(2,1)S(1)}, bf16[256,256]{1,0:T(8,128)(2,1)}, u32[]{:S(2)}) copy-start(bf16[256,256]{1,0:T(8,128)(2,1)} %param.9) | copy-start | bytes 393220
Sparse Core Ops, SparseCore 0:
  9.5 76.3 all-gather.3
  101.1 149.8 all-gather.5
  367.1 113.3 reduce-scatter.1
